TPU v7x, 32 devices: a whole 2x2x4 slice. The times are simulated.
32 devices in a mesh: rep: 4 (over x, core), stripe: 8 (over z, y).
Axes of the slice: x: 2, y: 2, z: 4, core: 2. Of those that a mesh axis runs over, the one named last changes fastest.
Arguments:
- activations: bfloat16 [1024, 1024], P('rep'), may hold values from -6 to 6
- out_grads: bfloat16 [1024, 4096], P('rep', 'stripe'), may hold values from -4 to 4
- statistics: float32 [4, 8, 512, 512], P('rep', 'stripe'), may hold values from -48 to 4608, as said below
- owner_blocks: int32 [8, 2], P('stripe'), may hold values from 0 to 1, each once within a row
Outputs:
- preconditioned: float32 [1024, 4096], P(None, 'stripe')
- new_stats: float32 [4, 8, 512, 512], P('rep', 'stripe')
Inputs may be any that keep to these rules, and one draw needn't show every extreme that they name: statistics[p, s] is symmetric positive definite for every p and s. `owner_blocks`: each row lists every row block 0 to 1 exactly once.
All inputs are finite; a program needn't handle non-finite values.
Results may differ from a plain program's by a relative error of at most 0.0003.
Values sent between devices are 32-bit elements; how exact they have to be, the bound alone decides.
No kernel may reach another device: no remote copies, remote signals or barrier semaphores. Data moves between devices by JAX's collectives and lax.ppermute only.
A program may use at most 128 MiB of HBM per device.

v0:
```python
import jax
import jax.numpy as jnp
from jax import lax
from jax.sharding import PartitionSpec as P

BLOCK = 512
ITERS = 2
decay_rate = 0.95
damping = 0.25
epsilon = 1e-06
highest = lax.Precision.HIGHEST


def partner(shard, axis, stride):
    return lax.ppermute(shard, axis, [(i, i ^ 1 << stride) for i in range(lax.axis_size(axis))])


def inverse_root(damped):
    identity = jnp.eye(damped.shape[-1], dtype=damped.dtype)
    frob_norm = jnp.sqrt(jnp.sum(damped * damped, axis=(-2, -1), keepdims=True) + epsilon)
    scaled = damped / frob_norm
    root_now = identity * frob_norm ** (-0.25)
    for sweep in range(ITERS):
        factor = (5.0 * identity - scaled) * 0.25
        root_now = jnp.matmul(root_now, factor, precision=highest)
        if sweep + 1 < ITERS:
            square = jnp.matmul(factor, factor, precision=highest)
            fourth = jnp.matmul(square, square, precision=highest)
            scaled = jnp.matmul(fourth, scaled, precision=highest)
    return root_now


def slot_terms(activations, out_grads, blocks_of, pair_count, piece_rows, row_count):
    tokens_here, in_width = activations.shape
    per_block = BLOCK // piece_rows
    shaped = activations.reshape(tokens_here, in_width // piece_rows, piece_rows)
    slot_count = row_count // piece_rows
    slot_ids = jnp.arange(slot_count, dtype=jnp.int32)
    block_ids = jnp.take(blocks_of, slot_ids % pair_count)
    half_ids = slot_ids // pair_count % per_block
    chosen = jnp.take(shaped, block_ids * per_block + half_ids, axis=1)
    products = jnp.einsum("tkp,tc->kpc", chosen, out_grads, preferred_element_type=jnp.float32)
    return products.reshape(slot_count * piece_rows, out_grads.shape[1])


def per_device(activations, out_grads, statistics, owner_blocks):
    rep_count = lax.axis_size("rep")
    pair_count = rep_count // 2
    pair_bit = rep_count.bit_length() - 2
    half_rows = BLOCK // 2
    my_index = lax.axis_index("rep")
    is_left = my_index < pair_count
    blocks_of = owner_blocks[0]
    own_half = lax.psum_scatter(
        slot_terms(
            activations,
            out_grads,
            blocks_of,
            pair_count,
            half_rows,
            half_rows * lax.axis_size("rep"),
        ),
        "rep",
        scatter_dimension=0,
        tiled=True,
    )
    partner_half = partner(own_half, "rep", pair_bit)
    gradient = jnp.where(
        is_left,
        jnp.concatenate([own_half, partner_half], axis=0),
        jnp.concatenate([partner_half, own_half], axis=0),
    )
    facing = jnp.where(is_left, gradient, gradient.T)
    new_stat = decay_rate * statistics[0, 0] + jnp.dot(facing, facing.T, precision=highest)
    trace_sum = lax.psum(jnp.trace(new_stat), ("rep", "stripe"))
    mean_diag = trace_sum / (rep_count * lax.axis_size("stripe") * BLOCK)
    identity = jnp.eye(BLOCK, dtype=jnp.float32)
    root_now = inverse_root(new_stat + damping * mean_diag * identity)
    partner_root = partner(root_now, "rep", pair_bit)
    left_root = jnp.where(is_left, root_now, partner_root)
    right_root = jnp.where(is_left, partner_root, root_now)
    row_start = jnp.where(is_left, 0, half_rows).astype(jnp.int32)
    my_rows = lax.dynamic_slice_in_dim(left_root, row_start, half_rows, 0)
    grad_rows = lax.dynamic_slice_in_dim(gradient, row_start, half_rows, 0)
    precond_half = jnp.dot(
        jnp.dot(my_rows, gradient, precision=highest), right_root, precision=highest
    )
    grad_sq, prec_sq = lax.psum(
        (jnp.sum(grad_rows * grad_rows), jnp.sum(precond_half * precond_half)), ("rep", "stripe")
    )
    scaled = precond_half * jnp.sqrt(grad_sq / (prec_sq + epsilon))
    gathered = lax.all_gather(scaled[None], "rep", axis=0, tiled=True)
    pair_ids = jnp.arange(pair_count, dtype=jnp.int32)
    inverse = jnp.sum(
        pair_ids[:, None] * (blocks_of[:, None] == pair_ids[None, :]).astype(jnp.int32), axis=0
    )
    row_order = jnp.stack([inverse, inverse + pair_count], axis=1).reshape(-1)
    preconditioned = jnp.take(gathered, row_order, axis=0).reshape(
        pair_count * BLOCK, gathered.shape[2]
    )
    return (preconditioned, new_stat[None, None])


def solution(mesh):
    in_specs = (
        P("rep", None),
        P("rep", "stripe"),
        P("rep", "stripe", None, None),
        P("stripe", None),
    )
    out_specs = (P(None, "stripe"), P("rep", "stripe", None, None))
    return jax.shard_map(
        per_device, mesh=mesh, in_specs=in_specs, out_specs=out_specs, check_vma=False
    )
```

profile of v0, /device:TPU:0, one launch (start us, length us, event | category | flops | bytes accessed | tf_op | source)
XLA Modules:
  0.0 226.6 jit_solution(13297253253330376592)
XLA Ops:
  8.2 1.3 gather_fusion
  9.6 1.2 copy.26
  12.2 1.8 copy.29
  14.1 34.0 %reduce-scatter.2.cloned.1.call-done = f32[256,512]{0,1:T(8,128)} async-done(((f32[1024,512]{0,1:T(8,128)}), f32[256,512]{0,1:T(8,128)}) %reduce-scatter.2.cloned.1.call-update) | async-done | bytes 524304 | tf_op jit(solution)/shard_map/reduce_scatter | solution.py:54
  48.5 13.4 %collective-permute-done = f32[256,512]{0,1:T(8,128)S(1)} collective-permute-done((f32[256,512]{0,1:T(8,128)}, f32[256,512]{0,1:T(8,128)S(1)}, u32[]{:S(2)}, u32[]{:S(2)}) %collective-permute-start) | collective-permute-done | bytes 524320 | tf_op jit(solution)/shard_map/ppermute | solution.py:15
  61.8 1.6 maximum_select_fusion
  63.8 5.6 %select_reduce_fusion = (f32[]{:T(128)}, f32[512,512]{1,0:T(8,128)S(1)}) fusion(f32[512,512]{1,0:T(8,128)S(1)} %copy.31, pred[]{:T(512)S(6)} %lt.75, f32[256,512]{0,1:T(8,128)} %reduce-scatter.2.cloned.1.call-done, f32[256,512]{0,1:T(8,128)} %copy-done.2, f32[1,1,512,512]{3,2,1,0:T(8,128)} %param.6), kind=kOutput, calls=%fused_computation.17 | convolution fusion | flops 1612972032 | bytes 4194309 | tf_op jit(solution)/shard_map/dot_general | solution.py:74
  69.4 39.7 %psum.21 = f32[]{:T(128)} all-reduce(f32[]{:T(128)} %get-tuple-element.4), channel_id=1, replica_groups=mesh['rep'=4,'stripe'=8] {'rep','stripe'}, use_global_device_ids=true, to_apply=%region_3.4 | all-reduce | flops 1 | bytes 8 | tf_op jit(solution)/shard_map/psum | solution.py:75
  109.6 1.0 multiply_reduce_fusion
  111.3 2.0 fusion.7
  113.4 1.9 fusion.4
  115.3 1.8 fusion.47
  117.2 1.9 fusion
  119.1 1.9 fusion.48
  121.0 2.3 %collective-permute-start.1 = (f32[512,512]{1,0:T(8,128)S(1)}, f32[512,512]{1,0:T(8,128)S(1)}, u32[]{:S(2)}, u32[]{:S(2)}) collective-permute-start(f32[512,512]{1,0:T(8,128)S(1)} %fusion.48), channel_id=1, source_target_pairs={{0,16},{8,24},{16,0},{24,8},{1,17},{9,25},{17,1},{25,9},{2,18},{10... | collective-permute-start | bytes 3145736 | tf_op jit(solution)/shard_map/ppermute | solution.py:15
  123.3 0.8 multiply_reduce_fusion.2
  124.1 21.7 %collective-permute-done.1 = f32[512,512]{1,0:T(8,128)S(1)} collective-permute-done((f32[512,512]{1,0:T(8,128)S(1)}, f32[512,512]{1,0:T(8,128)S(1)}, u32[]{:S(2)}, u32[]{:S(2)}) %collective-permute-start.1) | collective-permute-done | bytes 1048608 | tf_op jit(solution)/shard_map/ppermute | solution.py:15
  145.8 2.7 %fusion.10 = f32[256,512]{1,0:T(8,128)S(1)} fusion(f32[512,512]{1,0:T(8,128)S(1)} %collective-permute-done.1, s32[]{:T(128)S(6)} %select_n.184, f32[512,512]{1,0:T(8,128)S(1)} %fusion.48, pred[]{:T(512)S(6)} %lt.75, f32[256,512]{0,1:T(8,128)} %copy-done.2, f32[256,512]{0,1:T(8,128)} %reduce-scatter.2.cloned.1.call-done), kind=kOutput, calls=%fused_computation.22 | convolution fusion | flops 806223872 | bytes 2622976 | tf_op jit(solution)/shard_map/dot_general | solution.py:86
  148.5 1.8 multiply_reduce_fusion.1
  150.3 39.7 %all-reduce = (f32[]{:T(128)}, f32[]{:T(128)}) all-reduce(f32[]{:T(128)} %multiply_reduce_fusion.2, f32[]{:T(128)} %get-tuple-element.6), channel_id=1, replica_groups=mesh['rep'=4,'stripe'=8] {'rep','stripe'}, use_global_device_ids=true, to_apply=%region_6.7 | all-reduce | flops 2 | bytes 16 | tf_op jit(solution)/shard_map/psum | solution.py:88
  191.4 0.8 broadcast_multiply_fusion
  192.4 23.6 %all-gather.3.cloned.1.call-done = f32[1024,512]{1,0:T(8,128)} async-done(((f32[256,512]{1,0:T(8,128)}), f32[1024,512]{1,0:T(8,128)}) %all-gather.3.cloned.1.call-update) | async-done | bytes 2097168 | tf_op jit(solution)/shard_map/all_gather | solution.py:92
  216.0 2.3 %gather_fusion.2 = f32[4,256,512]{2,1,0:T(8,128)S(1)} fusion(f32[4,256,512]{2,1,0:T(8,128)} %bitcast.41, s32[1024]{0:T(1024)S(1)} %pad_clamp_fusion), kind=kCustom, calls=%fused_computation.2 | custom fusion | bytes 4194320 | tf_op jit(solution)/shard_map/jit(_take)/gather | solution.py:98
  218.2 1.5 bitcast_select_fusion
  (30 shorter events, 3.4 us)
Async XLA Ops:
  7.2 4.4 %copy-start = (bf16[256,512]{1,0:T(8,128)(2,1)S(1)}, bf16[256,512]{1,0:T(8,128)(2,1)}, u32[]{:S(2)}) copy-start(bf16[256,512]{1,0:T(8,128)(2,1)} %param.5) | copy-start | bytes 786436
  7.2 40.9 %reduce-scatter.2.cloned.1.call-start = ((), (), s32[]{:S(2)}) async-start(), calls=%async_computation.1 | async-start | bytes 2621440 | tf_op jit(solution)/shard_map/reduce_scatter | solution.py:54
  14.0 201.9 %all-gather.3.cloned.1.call-start = ((), (), s32[]{:S(2)}) async-start(), calls=%async_computation.2 | async-start | bytes 2621440 | tf_op jit(solution)/shard_map/all_gather | solution.py:92
  48.1 13.7 %collective-permute-start = (f32[256,512]{0,1:T(8,128)}, f32[256,512]{0,1:T(8,128)S(1)}, u32[]{:S(2)}, u32[]{:S(2)}) collective-permute-start(f32[256,512]{0,1:T(8,128)} %reduce-scatter.2.cloned.1.call-done), channel_id=1, source_target_pairs={{0,16},{8,24},{16,0},{24,8},{1,17},{9,25},{17,1},{25,9},{2,18},{10... | collective-permute-start | bytes 1572872 | tf_op jit(solution)/shard_map/ppermute | solution.py:15
  61.8 1.6 copy-start.2
  69.4 47.8 %copy-start.1 = (f32[512,512]{1,0:T(8,128)}, f32[512,512]{1,0:T(8,128)S(1)}, u32[]{:S(2)}) copy-start(f32[512,512]{1,0:T(8,128)S(1)} %get-tuple-element.5) | copy-start | bytes 3145732
  121.0 24.9 %collective-permute-start.1 = (f32[512,512]{1,0:T(8,128)S(1)}, f32[512,512]{1,0:T(8,128)S(1)}, u32[]{:S(2)}, u32[]{:S(2)}) collective-permute-start(f32[512,512]{1,0:T(8,128)S(1)} %fusion.48), channel_id=1, source_target_pairs={{0,16},{8,24},{16,0},{24,8},{1,17},{9,25},{17,1},{25,9},{2,18},{10... | collective-permute-start | bytes 3145736 | tf_op jit(solution)/shard_map/ppermute | solution.py:15
Sparse Core Ops, SparseCore 0:
  14.2 33.8 reduce-scatter.1
  192.3 23.5 all-gather.2
where the time goes:
time: 227 us
  waiting for transfers between devices  92.7 us (41%)
  blocking collectives  79.4 us (35%)
  matrix products  20.2 us (9%)
  between operations  16.9 us (7%)
  local copies, waits for them, and re-layouts  8.1 us (4%)
  other arithmetic  6.57 us (3%)
  starting transfers between devices  2.79 us (1%)
    psum x1, blocking collectives, per_device(): lax.psum((jnp.sum(grad_rows * grad_rows), jnp.sum(precond_half * precond_...  39.7 us
    psum x1, blocking collectives, per_device(): trace_sum = lax.psum(jnp.trace(new_stat), ('rep', 'stripe'))  39.7 us
    ppermute x2, waiting for transfers between devices, partner(): lax.ppermute(shard, axis, [(i, i ^ 1 << stride) for i in range(lax.axis_s...  35.1 us
    reduce_scatter x1, waiting for transfers between devices, per_device(): lax.psum_scatter(slot_terms(activations, out_grads, blocks_of, pair_count...  34 us
    all_gather x1, waiting for transfers between devices, per_device(): gathered = lax.all_gather(scaled[None], 'rep', axis=0, tiled=True)  23.6 us
    dot_general x1, matrix products, per_device(): jnp.dot(facing, facing.T, precision=highest)  5.62 us
  transfers between devices with their start and end apart: 4, of which 4 were waited for; matrix products, arithmetic and copies ran while one was open for 0% of the time, Pallas kernels for 0%

commit v1 on v0

--- a/solution.py
+++ b/solution.py
@@ -72,7 +72,7 @@
     )
     facing = jnp.where(is_left, gradient, gradient.T)
     new_stat = decay_rate * statistics[0, 0] + jnp.dot(facing, facing.T, precision=highest)
-    trace_sum = lax.psum(jnp.trace(new_stat), ("rep", "stripe"))
+    trace_sum = lax.all_gather(jnp.trace(new_stat), axis_name=("rep", "stripe")).sum(axis=0)
     mean_diag = trace_sum / (rep_count * lax.axis_size("stripe") * BLOCK)
     identity = jnp.eye(BLOCK, dtype=jnp.float32)
     root_now = inverse_root(new_stat + damping * mean_diag * identity)

time: 227 us -> 228 us (level)
    psum x1 -> x0, blocking collectives: 39.7 us -> none  [per_device(): trace_sum = lax.psum(jnp.trace(new_stat), ('rep', 'stripe'))]
    unnamed x0 -> x1, blocking collectives: none -> 39.4 us
where the time goes in v1:
time: 228 us
  waiting for transfers between devices  92.4 us (41%)
  blocking collectives  79.2 us (35%)
  matrix products  20.2 us (9%)
  between operations  17.1 us (8%)
  local copies, waits for them, and re-layouts  8.9 us (4%)
  other arithmetic  7.25 us (3%)
  starting transfers between devices  2.78 us (1%)
    psum x1, blocking collectives, per_device(): lax.psum((jnp.sum(grad_rows * grad_rows), jnp.sum(precond_half * precond_...  39.7 us
    unnamed x1, blocking collectives  39.4 us
    ppermute x2, waiting for transfers between devices, partner(): lax.ppermute(shard, axis, [(i, i ^ 1 << stride) for i in range(lax.axis_s...  34.9 us
    reduce_scatter x1, waiting for transfers between devices, per_device(): lax.psum_scatter(slot_terms(activations, out_grads, blocks_of, pair_count...  34 us
    all_gather x1, waiting for transfers between devices, per_device(): gathered = lax.all_gather(scaled[None], 'rep', axis=0, tiled=True)  23.5 us
    dot_general x1, matrix products, per_device(): jnp.dot(facing, facing.T, precision=highest)  5.62 us
  transfers between devices with their start and end apart: 4, of which 4 were waited for; matrix products, arithmetic and copies ran while one was open for 0% of the time, Pallas kernels for 0%

profile of v1, /device:TPU:0, one launch (start us, length us, event | category | flops | bytes accessed | tf_op | source)
XLA Modules:
  0.0 227.8 jit_solution(12759143974033136031)
XLA Ops:
  8.2 1.3 gather_fusion
  9.6 1.2 copy.26
  12.2 1.8 copy.29
  14.1 34.0 %reduce-scatter.2.cloned.1.call-done = f32[256,512]{0,1:T(8,128)} async-done(((f32[1024,512]{0,1:T(8,128)}), f32[256,512]{0,1:T(8,128)}) %reduce-scatter.2.cloned.1.call-update) | async-done | bytes 524304 | tf_op jit(solution)/shard_map/reduce_scatter | solution.py:54
  48.5 13.4 %collective-permute-done = f32[256,512]{0,1:T(8,128)S(1)} collective-permute-done((f32[256,512]{0,1:T(8,128)}, f32[256,512]{0,1:T(8,128)S(1)}, u32[]{:S(2)}, u32[]{:S(2)}) %collective-permute-start) | collective-permute-done | bytes 524320 | tf_op jit(solution)/shard_map/ppermute | solution.py:15
  61.8 1.6 maximum_select_fusion
  63.8 5.6 %select_reduce_fusion = (f32[]{:T(128)}, f32[512,512]{1,0:T(8,128)S(1)}) fusion(f32[512,512]{1,0:T(8,128)S(1)} %copy.31, pred[]{:T(512)S(6)} %lt.75, f32[256,512]{0,1:T(8,128)} %reduce-scatter.2.cloned.1.call-done, f32[256,512]{0,1:T(8,128)} %copy-done.2, f32[1,1,512,512]{3,2,1,0:T(8,128)} %param.6), kind=kOutput, calls=%fused_computation.17 | convolution fusion | flops 1612972032 | bytes 4194309 | tf_op jit(solution)/shard_map/dot_general | solution.py:74
  70.2 39.4 %all-reduce = f32[32]{0:T(128)S(1)} all-reduce(f32[32]{0:T(128)S(1)} %dynamic-update-slice), channel_id=1, replica_groups=mesh['rep'=4,'stripe'=8] {'rep','stripe'}, use_global_device_ids=true, to_apply=%add | all-reduce | flops 32 | bytes 256
  111.0 1.0 multiply_reduce_fusion
  112.7 2.0 fusion.7
  114.7 1.9 fusion.4
  116.7 1.8 fusion.47
  118.5 1.9 fusion
  120.4 1.9 fusion.48
  122.3 2.3 %collective-permute-start.1 = (f32[512,512]{1,0:T(8,128)S(1)}, f32[512,512]{1,0:T(8,128)S(1)}, u32[]{:S(2)}, u32[]{:S(2)}) collective-permute-start(f32[512,512]{1,0:T(8,128)S(1)} %fusion.48), channel_id=1, source_target_pairs={{0,16},{8,24},{16,0},{24,8},{1,17},{9,25},{17,1},{25,9},{2,18},{10... | collective-permute-start | bytes 3145736 | tf_op jit(solution)/shard_map/ppermute | solution.py:15
  124.6 0.8 multiply_reduce_fusion.2
  125.5 21.5 %collective-permute-done.1 = f32[512,512]{1,0:T(8,128)S(1)} collective-permute-done((f32[512,512]{1,0:T(8,128)S(1)}, f32[512,512]{1,0:T(8,128)S(1)}, u32[]{:S(2)}, u32[]{:S(2)}) %collective-permute-start.1) | collective-permute-done | bytes 1048608 | tf_op jit(solution)/shard_map/ppermute | solution.py:15
  147.0 2.7 %fusion.10 = f32[256,512]{1,0:T(8,128)S(1)} fusion(f32[512,512]{1,0:T(8,128)S(1)} %collective-permute-done.1, s32[]{:T(128)S(6)} %select_n.184, f32[512,512]{1,0:T(8,128)S(1)} %fusion.48, pred[]{:T(512)S(6)} %lt.75, f32[256,512]{0,1:T(8,128)} %copy-done.2, f32[256,512]{0,1:T(8,128)} %reduce-scatter.2.cloned.1.call-done), kind=kOutput, calls=%fused_computation.22 | convolution fusion | flops 806223872 | bytes 2622976 | tf_op jit(solution)/shard_map/dot_general | solution.py:86
  149.7 1.8 multiply_reduce_fusion.1
  151.4 39.7 %all-reduce.1 = (f32[]{:T(128)}, f32[]{:T(128)}) all-reduce(f32[]{:T(128)} %multiply_reduce_fusion.2, f32[]{:T(128)} %get-tuple-element.6), channel_id=1, replica_groups=mesh['rep'=4,'stripe'=8] {'rep','stripe'}, use_global_device_ids=true, to_apply=%region_6.7 | all-reduce | flops 2 | bytes 16 | tf_op jit(solution)/shard_map/psum | solution.py:88
  192.5 0.8 broadcast_multiply_fusion
  193.6 23.5 %all-gather.3.cloned.1.call-done = f32[1024,512]{1,0:T(8,128)} async-done(((f32[256,512]{1,0:T(8,128)}), f32[1024,512]{1,0:T(8,128)}) %all-gather.3.cloned.1.call-update) | async-done | bytes 2097168 | tf_op jit(solution)/shard_map/all_gather | solution.py:92
  217.1 2.3 gather_fusion.2
  219.4 1.5 bitcast_select_fusion
  (33 shorter events, 4.9 us)
Async XLA Ops:
  7.2 4.4 %copy-start = (bf16[256,512]{1,0:T(8,128)(2,1)S(1)}, bf16[256,512]{1,0:T(8,128)(2,1)}, u32[]{:S(2)}) copy-start(bf16[256,512]{1,0:T(8,128)(2,1)} %param.5) | copy-start | bytes 786436
  7.2 40.9 %reduce-scatter.2.cloned.1.call-start = ((), (), s32[]{:S(2)}) async-start(), calls=%async_computation.1 | async-start | bytes 2621440 | tf_op jit(solution)/shard_map/reduce_scatter | solution.py:54
  14.0 203.1 %all-gather.3.cloned.1.call-start = ((), (), s32[]{:S(2)}) async-start(), calls=%async_computation.2 | async-start | bytes 2621440 | tf_op jit(solution)/shard_map/all_gather | solution.py:92
  48.1 13.7 %collective-permute-start = (f32[256,512]{0,1:T(8,128)}, f32[256,512]{0,1:T(8,128)S(1)}, u32[]{:S(2)}, u32[]{:S(2)}) collective-permute-start(f32[256,512]{0,1:T(8,128)} %reduce-scatter.2.cloned.1.call-done), channel_id=1, source_target_pairs={{0,16},{8,24},{16,0},{24,8},{1,17},{9,25},{17,1},{25,9},{2,18},{10... | collective-permute-start | bytes 1572872 | tf_op jit(solution)/shard_map/ppermute | solution.py:15
  61.8 1.6 copy-start.2
  69.4 49.1 %copy-start.1 = (f32[512,512]{1,0:T(8,128)}, f32[512,512]{1,0:T(8,128)S(1)}, u32[]{:S(2)}) copy-start(f32[512,512]{1,0:T(8,128)S(1)} %get-tuple-element.5) | copy-start | bytes 3145732
  122.3 24.7 %collective-permute-start.1 = (f32[512,512]{1,0:T(8,128)S(1)}, f32[512,512]{1,0:T(8,128)S(1)}, u32[]{:S(2)}, u32[]{:S(2)}) collective-permute-start(f32[512,512]{1,0:T(8,128)S(1)} %fusion.48), channel_id=1, source_target_pairs={{0,16},{8,24},{16,0},{24,8},{1,17},{9,25},{17,1},{25,9},{2,18},{10... | collective-permute-start | bytes 3145736 | tf_op jit(solution)/shard_map/ppermute | solution.py:15
Sparse Core Ops, SparseCore 0:
  14.2 33.8 reduce-scatter.1
  193.5 23.5 all-gather.2
